TPU v7x, 256 devices: a whole 4x4x8 slice. The times are simulated.
256 devices in a mesh: seq: 16 (over z, core), tp: 16 (over y, x).
Axes of the slice: x: 4, y: 4, z: 8, core: 2. Of those that a mesh axis runs over, the one named last changes fastest.
Arguments:
- tokens: bfloat16 [8192, 4096], P('seq', 'tp'), may hold values from -60 to 60
- w_qkv: bfloat16 [4096, 3, 4096], P(None, None, 'tp'), may hold values from -0.09375 to 0.09375
- w_out: bfloat16 [4096, 4096], P('tp'), may hold values from -0.09375 to 0.09375
- rand_blocks: int32 [128, 32, 3], P('seq', 'tp'), may hold values from 0 to 127, as said below
- glob_blocks: int32 [2], replicated, may hold values from 0 to 127, as said below
- window_radius: int32 [32], P('tp'), may hold values from 0 to 1, as said below
Outputs:
- mixed: bfloat16 [8192, 4096], P('seq', 'tp')
Inputs may be any that keep to these rules, and one draw needn't show every extreme that they name: `rand_blocks`: split the blocks into aligned runs of 8 blocks. For one head and the query blocks of one run, the 24 entries lie at most C = ceil(8 * 3 / 16) times in any one run, and exactly C times in some run. `glob_blocks`: the 2 ids are distinct; the last block, 127, is always one of them. `window_radius`: some head has radius 1.
All inputs are finite; a program needn't handle non-finite values.
Results may differ from a plain program's by a relative error of at most 0.033.
Values may be sent and summed in bfloat16 or wider, within the bound.
No kernel may reach another device: no remote copies, remote signals or barrier semaphores. Data moves between devices by JAX's collectives and lax.ppermute only.
A program may use at most 128 MiB of HBM per device.

v0:
```python
import math
import jax
import jax.numpy as jnp
from jax import lax
from jax.sharding import PartitionSpec as P

DH = 128
BLK = 64
big_negative = -1e30


def padded_2(block, sides, width):
    for axis, dim in sides:
        count = lax.axis_size(axis)
        forward = [(i, i + 1) for i in range(count - 1)]
        backward = [(target, source) for source, target in forward]
        low = lax.ppermute(
            lax.slice_in_dim(block, block.shape[dim] - width, None, axis=dim), axis, forward
        )
        high = lax.ppermute(lax.slice_in_dim(block, 0, width, axis=dim), axis, backward)
        block = jnp.concatenate([low, block, high], axis=dim)
    return block


def body(tokens, w_qkv, w_out, rand_blocks, glob_blocks, window_radius):
    tok_rows = tokens.shape[0]
    local_blocks = tok_rows // BLK
    head_cols = w_qkv.shape[2]
    local_heads = head_cols // DH
    shard_count = lax.axis_size("seq")
    total_blocks = local_blocks * shard_count
    glob_count = glob_blocks.shape[0]
    scale = 1.0 / math.sqrt(DH)
    projected = jnp.einsum(
        "tf,fcj->ctj",
        lax.all_gather(tokens, "tp", axis=1, tiled=True),
        w_qkv,
        preferred_element_type=jnp.float32,
    )
    projected = projected.astype(jnp.bfloat16)
    query = projected[0].reshape(local_blocks, BLK, local_heads, DH)
    key_value = projected[1:]
    padded = padded_2(key_value, (("seq", 1),), BLK)
    padded_blocks = padded.reshape(2, local_blocks + 2, BLK, local_heads, DH)
    nearby = jnp.stack(
        [padded_blocks[:, offset : offset + local_blocks] for offset in range(3)], axis=2
    )
    my_shard = lax.axis_index("seq")
    first_block = my_shard * local_blocks
    block_ids = first_block + jnp.arange(local_blocks, dtype=jnp.int32)
    offsets = jnp.arange(3, dtype=jnp.int32) - 1
    targets = block_ids[:, None] + offsets[None, :]
    in_range = (targets >= 0) & (targets < total_blocks)
    near_valid = in_range[:, None, :] & (
        jnp.abs(offsets)[None, None, :] <= window_radius[None, :, None]
    )
    scores = (
        jnp.einsum("nqhd,nwkhd->nhqwk", query, nearby[0], preferred_element_type=jnp.float32)
        * scale
    )
    scores = jnp.where(near_valid[:, :, None, :, None], scores, big_negative)
    row_max = jnp.max(scores, axis=(3, 4))
    weights = jnp.exp(scores - row_max[..., None, None])
    row_sum = jnp.sum(weights, axis=(3, 4))
    accum = jnp.einsum(
        "nhqwk,nwkhd->nhqd",
        weights.astype(jnp.bfloat16),
        nearby[1],
        preferred_element_type=jnp.float32,
    )
    listed = jnp.concatenate(
        [
            rand_blocks,
            jnp.broadcast_to(glob_blocks[None, None, :], (local_blocks, local_heads, glob_count)),
        ],
        axis=2,
    )
    glob_local = glob_blocks - first_block
    glob_clip = jnp.clip(glob_local, 0, local_blocks - 1)
    glob_query = query[glob_clip]
    head_index = jnp.arange(local_heads, dtype=jnp.int32)[None, :, None]
    gathered = lax.all_gather(key_value, "seq", axis=1, tiled=True)
    list_sum = row_sum
    list_acc = accum
    dense_max = jnp.full((glob_count, local_heads, BLK), big_negative, jnp.float32)
    piece_rows = gathered.shape[1]
    piece_blocks = piece_rows // BLK
    key_blocks = gathered.reshape(2, piece_blocks, BLK, local_heads, DH)
    relative = listed - 0 // BLK
    inside = (relative >= 0) & (relative < piece_blocks)
    clipped = jnp.clip(relative, 0, piece_blocks - 1)
    keys_taken = key_blocks[0][clipped, :, head_index, :]
    values_taken = key_blocks[1][clipped, :, head_index, :]
    chosen = (
        jnp.einsum("nqhd,nhskd->nhqsk", query, keys_taken, preferred_element_type=jnp.float32)
        * scale
    )
    chosen = jnp.where(inside[:, :, None, :, None], chosen, big_negative)
    new_max = jnp.maximum(row_max, jnp.max(chosen, axis=(3, 4)))
    factor = jnp.exp(row_max - new_max)
    probs = jnp.exp(chosen - new_max[..., None, None])
    list_sum = list_sum * factor + jnp.sum(probs, axis=(3, 4))
    list_acc = list_acc * factor[..., None] + jnp.einsum(
        "nhqsk,nhskd->nhqd",
        probs.astype(jnp.bfloat16),
        values_taken,
        preferred_element_type=jnp.float32,
    )
    flat_keys = gathered[0].reshape(piece_rows, local_heads, DH)
    flat_values = gathered[1].reshape(piece_rows, local_heads, DH)
    dense = (
        jnp.einsum("gqhd,khd->ghqk", glob_query, flat_keys, preferred_element_type=jnp.float32)
        * scale
    )
    dense_new = jnp.maximum(dense_max, jnp.max(dense, axis=3))
    dense_probs = jnp.exp(dense - dense_new[..., None])
    dense_sum = jnp.sum(dense_probs, axis=3)
    dense_acc = jnp.einsum(
        "ghqk,khd->ghqd",
        dense_probs.astype(jnp.bfloat16),
        flat_values,
        preferred_element_type=jnp.float32,
    )
    attended = list_acc / list_sum[..., None]
    dense_out = dense_acc / dense_sum[..., None]
    for which in range(glob_count):
        owned_block = (block_ids == glob_blocks[which])[:, None, None, None]
        attended = jnp.where(owned_block, dense_out[which][None], attended)
    attended = attended.astype(jnp.bfloat16).transpose(0, 2, 1, 3).reshape(tok_rows, head_cols)
    partial_terms = jnp.dot(attended, w_out, preferred_element_type=jnp.float32)
    return lax.psum_scatter(
        partial_terms.astype(jnp.bfloat16), "tp", scatter_dimension=1, tiled=True
    )


def solution(mesh):
    return jax.shard_map(
        body,
        mesh=mesh,
        in_specs=(
            P("seq", "tp"),
            P(None, None, "tp"),
            P("tp", None),
            P("seq", "tp", None),
            P(),
            P("tp"),
        ),
        out_specs=P("seq", "tp"),
        check_vma=False,
    )
```

profile of v0, /device:TPU:2, one launch (start us, length us, event | category | flops | bytes accessed | tf_op | source)
XLA Modules:
  0.0 310.6 jit_solution(3259309802515597309)
XLA Ops:
  7.3 67.7 %all-gather.3.cloned.1.call-done = bf16[512,4096]{1,0:T(8,128)(2,1)} async-done(((bf16[512,256]{1,0:T(8,128)(2,1)}), bf16[512,4096]{1,0:T(8,128)(2,1)}) %all-gather.3.cloned.1.call-update) | async-done | bytes 4194320 | tf_op jit(solution)/shard_map/all_gather | solution.py:36
  75.0 7.5 %fusion.22 = bf16[3,512,256]{1,2,0:T(8,128)(2,1)S(1)} fusion(bf16[4096,3,256]{2,0,1:T(8,128)(2,1)} %param.7, bf16[512,4096]{1,0:T(8,128)(2,1)} %all-gather.3.cloned.1.call-done), kind=kOutput, calls=%fused_computation.29 | convolution fusion | flops 3221618688 | bytes 11272192 | tf_op jit(solution)/shard_map/tf,fcj->ctj/dot_general | solution.py:34
  85.8 1.7 fusion.76
  87.5 1.9 collective-permute-start
  89.4 1.3 collective-permute-start.1
  90.7 1.9 broadcast_compare_fusion.1
  95.0 1.4 pad_maximum_fusion.1
  97.6 1.9 reshape.176
  103.2 36.9 %all-gather.5.cloned.1.call-done = bf16[2,8192,256]{1,2,0:T(8,128)(2,1)} async-done(((bf16[2,512,256]{1,2,0:T(8,128)(2,1)}), bf16[2,8192,256]{1,2,0:T(8,128)(2,1)}) %all-gather.5.cloned.1.call-update) | async-done | bytes 8388624 | tf_op jit(solution)/shard_map/all_gather | solution.py:82
  140.1 5.9 %fusion.75 = (bf16[1,8192,256]{1,2,0:T(8,128)(2,1)}, bf16[1,8192,256]{1,2,0:T(8,128)(2,1)}) fusion(bf16[2,8192,256]{1,2,0:T(8,128)(2,1)} %all-gather.5.cloned.1.call-done), kind=kLoop, calls=%fused_computation.87 | loop fusion | bytes 16777216 | tf_op jit(solution)/shard_map/slice | solution.py:110
  146.1 12.6 %reshape.208 = bf16[128,64,2,128]{1,0,3,2:T(8,128)(2,1)} reshape(bf16[1,8192,256]{1,2,0:T(8,128)(2,1)} %get-tuple-element.8) | data formatting | bytes 8388608 | tf_op jit(solution)/shard_map/squeeze | solution.py:92
  158.7 3.4 %fusion.79 = f32[2,8192,128]{1,2,0:S(1)} fusion(bf16[2,128,128]{1,2,0:T(8,128)(2,1)S(1)} %bitcast.134, bf16[8192,2,128]{0,2,1:T(8,128)(2,1)} %bitcast.123), kind=kOutput, calls=%fused_computation.91 | convolution fusion | flops 536870912 | bytes 12648448
  162.9 2.4 copy-done.1
  165.3 1.5 fusion.1
  166.9 12.6 %reshape.209 = bf16[128,64,2,128]{1,0,3,2:T(8,128)(2,1)} reshape(bf16[1,8192,256]{1,2,0:T(8,128)(2,1)} %get-tuple-element.7) | data formatting | bytes 8388608 | tf_op jit(solution)/shard_map/squeeze | solution.py:93
  179.4 6.3 %fusion.49 = bf16[2,2,64,128]{3,2,0,1:T(8,128)(2,1)S(1)} fusion(bf16[8192,2,128,1]{0,2,3,1:T(8,128)(2,1)} %bitcast.124, f32[2,8192,2,64]{1,3,2,0:T(8,128)} %bitcast.122, f32[2,2,64]{2,0,1:T(2,128)S(1)} %broadcast_maximum_fusion, f32[2,2,64]{2,0,1:T(2,128)S(1)} %fusion.1), kind=kOutput, calls=%fused_computation.41 | convolution fusion | flops 543227904 | bytes 12650496 | tf_op jit(solution)/shard_map/ghqk,khd->ghqd/dot_general | solution.py:118
  185.7 10.5 %copy.39 = bf16[128,64,2,128]{3,1,2,0:T(8,128)(2,1)} copy(bf16[128,64,2,128]{1,0,3,2:T(8,128)(2,1)} %reshape.209) | data formatting | bytes 8388608 | tf_op jit(solution)/shard_map/squeeze | solution.py:93
  196.2 10.5 %copy.36 = bf16[128,64,2,128]{3,1,2,0:T(8,128)(2,1)} copy(bf16[128,64,2,128]{1,0,3,2:T(8,128)(2,1)} %reshape.208) | data formatting | bytes 8388608 | tf_op jit(solution)/shard_map/squeeze | solution.py:92
  206.7 4.5 %gather_fusion.2 = bf16[80,64,128]{2,1,0:T(8,128)(2,1)} fusion(bf16[128,64,2,128]{3,1,2,0:T(8,128)(2,1)} %copy.39, s32[80]{0:T(128)S(1)} %reshape.186), kind=kCustom, calls=%fused_computation.2 | custom fusion | bytes 2622080 | tf_op jit(solution)/shard_map/gather | solution.py:93
  211.2 3.4 %gather_fusion.1 = bf16[80,64,128]{2,1,0:T(8,128)(2,1)S(1)} fusion(bf16[128,64,2,128]{3,1,2,0:T(8,128)(2,1)} %copy.36, s32[80]{0:T(128)S(1)} %reshape.186), kind=kCustom, calls=%fused_computation.1 | custom fusion | bytes 2622080 | tf_op jit(solution)/shard_map/gather | solution.py:92
  214.6 1.7 fusion.9
  218.2 1.2 fusion.46
  219.8 3.2 %convolution_convert_fusion = bf16[512,4096]{1,0:T(8,128)(2,1)} fusion(bf16[256,4096]{1,0:T(8,128)(2,1)S(1)} %copy-done, bf16[64,8,2,128]{3,2,1,0:T(2,128)(2,1)S(1)} %bitcast.133), kind=kOutput, calls=%fused_computation.8 | convolution fusion | flops 1075838976 | bytes 6553600 | tf_op jit(solution)/shard_map/dot_general | solution.py:130
  223.0 81.1 %reduce-scatter.2.cloned.1.call-done = bf16[512,256]{1,0:T(8,128)(2,1)} async-done(((bf16[512,4096]{1,0:T(8,128)(2,1)}), bf16[512,256]{1,0:T(8,128)(2,1)}) %reduce-scatter.2.cloned.1.call-update) | async-done | bytes 262160 | tf_op jit(solution)/shard_map/reduce_scatter | solution.py:131
  (78 shorter events, 14.1 us)
Async XLA Ops:
  6.5 213.2 %copy-start = (bf16[256,4096]{1,0:T(8,128)(2,1)S(1)}, bf16[256,4096]{1,0:T(8,128)(2,1)}, u32[]{:S(2)}) copy-start(bf16[256,4096]{1,0:T(8,128)(2,1)} %param.8) | copy-start | bytes 6291460
  6.5 68.5 %all-gather.3.cloned.1.call-start = ((), (), s32[]{:S(2)}) async-start(), calls=%async_computation.1 | async-start | bytes 4456448 | tf_op jit(solution)/shard_map/all_gather | solution.py:36
  7.3 77.1 %copy-start.12 = (s32[2]{0:T(128)S(1)}, s32[2]{0:T(128)}, u32[]{:S(2)}) copy-start(s32[2]{0:T(128)} %param.10) | copy-start | bytes 28
  7.3 77.2 %copy-start.11 = (s32[8,2,3]{0,1,2:T(2,128)S(1)}, s32[8,2,3]{0,1,2:T(2,128)}, u32[]{:S(2)}) copy-start(s32[8,2,3]{0,1,2:T(2,128)} %param.9) | copy-start | bytes 580
  7.3 78.3 %copy-start.15 = (s32[2]{0:T(128)S(1)}, s32[2]{0:T(128)}, u32[]{:S(2)}) copy-start(s32[2]{0:T(128)} %param.11) | copy-start | bytes 28
  7.3 132.8 %all-gather.5.cloned.1.call-start = ((), (), s32[]{:S(2)}) async-start(), calls=%async_computation.2 | async-start | bytes 8912896 | tf_op jit(solution)/shard_map/all_gather | solution.py:82
  82.5 1.0 copy-start.8
  84.3 10.7 %copy-start.4 = (bf16[2,512,256]{1,2,0:T(8,128)(2,1)S(1)}, bf16[2,512,256]{1,2,0:T(8,128)(2,1)}, u32[]{:S(2)}) copy-start(bf16[2,512,256]{1,2,0:T(8,128)(2,1)} %slice.72) | copy-start | bytes 1572868
  84.3 219.8 %reduce-scatter.2.cloned.1.call-start = ((), (), s32[]{:S(2)}) async-start(), calls=%async_computation.3 | async-start | bytes 4456448 | tf_op jit(solution)/shard_map/reduce_scatter | solution.py:131
  87.5 7.5 %collective-permute-start = (bf16[2,64,256]{1,2,0:T(8,128)(2,1)}, bf16[2,64,256]{1,2,0:T(8,128)(2,1)}, u32[]{:S(2)}, u32[]{:S(2)}) collective-permute-start(bf16[2,64,256]{1,2,0:T(8,128)(2,1)} %get-tuple-element.9), channel_id=1, source_target_pairs={{0,16},{16,32},{32,48},{48,64},{64,80},{80,96},{96,112},{112,128},... | collective-permute-start | bytes 196616 | tf_op jit(solution)/shard_map/ppermute | solution.py:17
  89.4 5.6 %collective-permute-start.1 = (bf16[2,64,256]{1,2,0:T(8,128)(2,1)S(1)}, bf16[2,64,256]{1,2,0:T(8,128)(2,1)}, u32[]{:S(2)}, u32[]{:S(2)}) collective-permute-start(bf16[2,64,256]{1,2,0:T(8,128)(2,1)S(1)} %get-tuple-element.10), channel_id=1, source_target_pairs={{16,0},{32,16},{48,32},{64,48},{80,64},{96,80},{112,96},{128,112},... | collective-permute-start | bytes 196616 | tf_op jit(solution)/shard_map/ppermute | solution.py:20
  93.8 7.4 %copy-start.5 = (bf16[8,64,2,128]{3,2,1,0:T(2,128)(2,1)}, bf16[8,64,2,128]{3,2,1,0:T(2,128)(2,1)S(1)}, u32[]{:S(2)}) copy-start(bf16[8,64,2,128]{3,2,1,0:T(2,128)(2,1)S(1)} %reshape_squeeze.11) | copy-start | bytes 786436
  101.1 1.2 copy-start.6
  101.5 1.2 copy-start.2
  146.1 12.6 %copy-start.10 = (bf16[2,64,2,128]{3,1,0,2:T(8,128)(2,1)S(1)}, bf16[2,64,2,128]{3,1,0,2:T(8,128)(2,1)}, u32[]{:S(2)}) copy-start(bf16[2,64,2,128]{3,1,0,2:T(8,128)(2,1)} %copy.25) | copy-start | bytes 196612
  162.1 3.2 %copy-start.1 = (f32[2,8192,128]{1,2,0}, f32[2,8192,128]{1,2,0:S(1)}, u32[]{:S(2)}) copy-start(f32[2,8192,128]{1,2,0:S(1)} %fusion.79) | copy-start | bytes 25165828
  214.6 2.6 copy-start.3
  214.6 2.6 copy-start.7
  216.4 1.8 copy-start.9
  216.4 1.8 copy-start.13
  216.4 1.8 copy-start.14
Sparse Core Ops, SparseCore 0:
  9.8 65.2 all-gather.2
  84.4 55.6 all-gather.4
  223.1 80.8 reduce-scatter.1
where the time goes:
time: 312 us; the launch traced here: 311 us
  waiting for transfers between devices  186 us (60%)
  local copies, waits for them, and re-layouts  75 us (24%)
  matrix products  24.7 us (8%)
  between operations  13.5 us (4%)
  other arithmetic  7.69 us (2%)
  starting transfers between devices  3.3 us (1%)
    reduce_scatter x1, waiting for transfers between devices, body(): lax.psum_scatter(partial_terms.astype(jnp.bfloat16), 'tp', scatter_dimens...  81.1 us
    all_gather x1, waiting for transfers between devices, body(): lax.all_gather(tokens, 'tp', axis=1, tiled=True)  67.7 us
    all_gather x1, waiting for transfers between devices, body(): gathered = lax.all_gather(key_value, 'seq', axis=1, tiled=True)  36.9 us
    squeeze x2, local copies, waits for them, and re-layouts, body(): keys_taken = key_blocks[0][clipped, :, head_index, :]  23.1 us
    squeeze x2, local copies, waits for them, and re-layouts, body(): values_taken = key_blocks[1][clipped, :, head_index, :]  23 us
    dot_general x1, matrix products, body(): jnp.einsum('tf,fcj->ctj', lax.all_gather(tokens, 'tp', axis=1, tiled=True...  7.46 us
    dot_general x1, matrix products, body(): jnp.einsum('ghqk,khd->ghqd', dense_probs.astype(jnp.bfloat16), flat_value...  6.28 us
  transfers between devices with their start and end apart: 5, of which 3 were waited for; matrix products, arithmetic and copies ran while one was open for 5% of the time, Pallas kernels for 0%

commit v1 on v0

--- a/solution.py
+++ b/solution.py
@@ -79,7 +79,9 @@
     glob_clip = jnp.clip(glob_local, 0, local_blocks - 1)
     glob_query = query[glob_clip]
     head_index = jnp.arange(local_heads, dtype=jnp.int32)[None, :, None]
-    gathered = lax.all_gather(key_value, "seq", axis=1, tiled=True)
+    gathered = jnp.concatenate(
+        lax.all_to_all(jnp.stack([key_value] * lax.axis_size("seq")), "seq", 0, 0), axis=1
+    )
     list_sum = row_sum
     list_acc = accum
     dense_max = jnp.full((glob_count, local_heads, BLK), big_negative, jnp.float32)

time: 312 us -> 446 us (1.43)
  waiting for transfers between devices: 186 us -> 324 us
  starting transfers between devices: 3.3 us -> 11.6 us
  local copies, waits for them, and re-layouts: 75 us -> 67.3 us
    all_to_all x0 -> x1, waiting for transfers between devices: none -> 164 us  [body(): lax.all_to_all(jnp.stack([key_value] * lax.axis_size('seq')), 'seq', 0, 0)]
    all_gather x1 -> x0, waiting for transfers between devices: 36.9 us -> none  [body(): gathered = lax.all_gather(key_value, 'seq', axis=1, tiled=True)]
    another operation x0 -> x3, local copies, waits for them, and re-layouts: none -> 18 us  [the longest x1 6.92 us: body(): flat_keys = gathered[0].reshape(piece_rows, local_heads, DH)]
    squeeze x2, local copies, waits for them, and re-layouts: 23 us -> 10.2 us  [body(): values_taken = key_blocks[1][clipped, :, head_index, :]]
    reduce_scatter x1, waiting for transfers between devices: 81.1 us -> 91.8 us  [body(): lax.psum_scatter(partial_terms.astype(jnp.bfloat16), 'tp', scatter_dimens...]
    squeeze x2, local copies, waits for them, and re-layouts: 23.1 us -> 12.3 us  [body(): keys_taken = key_blocks[0][clipped, :, head_index, :]]
    all_to_all x0 -> x1, starting transfers between devices: none -> 7.31 us  [body(): lax.all_to_all(jnp.stack([key_value] * lax.axis_size('seq')), 'seq', 0, 0)]
  transfers between devices with their start and end apart: 5 -> 5, of which waited for: 3 -> 3; matrix products, arithmetic and copies ran while one was open for 5% -> 3% of each run, Pallas kernels for 0% -> 0%
where the time goes in v1:
time: 446 us; the launch traced here: 445 us
  waiting for transfers between devices  324 us (73%)
  local copies, waits for them, and re-layouts  67.3 us (15%)
  matrix products  20.8 us (5%)
  between operations  13.8 us (3%)
  starting transfers between devices  11.6 us (3%)
  other arithmetic  7.91 us (2%)
    all_to_all x1, waiting for transfers between devices, body(): lax.all_to_all(jnp.stack([key_value] * lax.axis_size('seq')), 'seq', 0, 0)  164 us
    reduce_scatter x1, waiting for transfers between devices, body(): lax.psum_scatter(partial_terms.astype(jnp.bfloat16), 'tp', scatter_dimens...  91.8 us
    all_gather x1, waiting for transfers between devices, body(): lax.all_gather(tokens, 'tp', axis=1, tiled=True)  67.8 us
    squeeze x2, local copies, waits for them, and re-layouts, body(): keys_taken = key_blocks[0][clipped, :, head_index, :]  12.3 us
    squeeze x2, local copies, waits for them, and re-layouts, body(): values_taken = key_blocks[1][clipped, :, head_index, :]  10.2 us
  transfers between devices with their start and end apart: 5, of which 3 were waited for; matrix products, arithmetic and copies ran while one was open for 3% of the time, Pallas kernels for 0%

profile of v1, /device:TPU:2, one launch (start us, length us, event | category | flops | bytes accessed | tf_op | source)
XLA Modules:
  0.0 445.2 jit_solution(1886742238132062184)
XLA Ops:
  7.3 67.8 %all-gather.2.cloned.1.call-done = bf16[512,4096]{1,0:T(8,128)(2,1)} async-done(((bf16[512,256]{1,0:T(8,128)(2,1)}), bf16[512,4096]{1,0:T(8,128)(2,1)}) %all-gather.2.cloned.1.call-update) | async-done | bytes 4194320 | tf_op jit(solution)/shard_map/all_gather | solution.py:36
  75.0 7.5 %fusion.25 = bf16[3,512,256]{1,2,0:T(8,128)(2,1)S(1)} fusion(bf16[4096,3,256]{2,0,1:T(8,128)(2,1)} %param.7, bf16[512,4096]{1,0:T(8,128)(2,1)} %all-gather.2.cloned.1.call-done), kind=kOutput, calls=%fused_computation.32 | convolution fusion | flops 3221618688 | bytes 11272192 | tf_op jit(solution)/shard_map/tf,fcj->ctj/dot_general | solution.py:34
  83.6 4.2 stack.10
  87.8 7.3 %all-to-all-start = ((bf16[16,2,512,256]{3,2,1,0:T(8,128)(2,1)}), bf16[16,2,512,256]{3,2,1,0:T(8,128)(2,1)}, u32[]{:S(2)}, u32[]{:S(2)}) async-start(bf16[16,2,512,256]{3,2,1,0:T(8,128)(2,1)} %stack.10), calls=%async_computation | async-start | bytes 16777216 | tf_op jit(solution)/shard_map/all_to_all | solution.py:83
  97.3 2.9 collective-permute-start
  105.4 2.2 pad_maximum_fusion.1
  107.6 2.2 copy.66
  109.7 1.9 reshape.186
  115.9 163.5 %all-to-all-done = bf16[16,2,512,256]{3,2,1,0:T(8,128)(2,1)} async-done(((bf16[16,2,512,256]{3,2,1,0:T(8,128)(2,1)}), bf16[16,2,512,256]{3,2,1,0:T(8,128)(2,1)}, u32[]{:S(2)}, u32[]{:S(2)}) %all-to-all-start) | async-done | bytes 8388640 | tf_op jit(solution)/shard_map/all_to_all | solution.py:83
  279.4 5.8 %fusion.82 = (bf16[1,16,512,256]{3,2,0,1:T(8,128)(2,1)}, bf16[1,16,512,256]{3,2,0,1:T(8,128)(2,1)}) fusion(bf16[2,16,512,256]{3,2,0,1:T(8,128)(2,1)} %bitcast.3), kind=kLoop, calls=%fused_computation.90 | loop fusion | bytes 16777216 | tf_op jit(solution)/shard_map/slice | solution.py:112
  285.2 6.9 %squeeze.22 = bf16[128,64,2,128]{3,2,1,0:T(2,128)(2,1)} reshape(bf16[1,16,512,256]{3,2,0,1:T(8,128)(2,1)} %get-tuple-element.8) | data formatting | bytes 8388608 | tf_op jit(solution)/shard_map/squeeze | solution.py:94
  292.1 6.9 %reshape.219 = bf16[8192,2,128]{2,1,0:T(2,128)(2,1)} reshape(bf16[1,16,512,256]{3,2,0,1:T(8,128)(2,1)} %get-tuple-element.8) | data formatting | bytes 8388608 | tf_op jit(solution)/shard_map/reshape;squeeze | solution.py:111
  299.0 6.9 %reshape.218 = bf16[8192,2,128]{2,1,0:T(2,128)(2,1)} reshape(bf16[1,16,512,256]{3,2,0,1:T(8,128)(2,1)} %get-tuple-element.7) | data formatting | bytes 8388608 | tf_op jit(solution)/shard_map/reshape;squeeze | solution.py:112
  305.9 7.0 %squeeze.23 = bf16[128,64,2,128]{3,2,1,0:T(2,128)(2,1)} reshape(bf16[1,16,512,256]{3,2,0,1:T(8,128)(2,1)} %get-tuple-element.7) | data formatting | bytes 8388608 | tf_op jit(solution)/shard_map/squeeze | solution.py:95
  312.9 5.4 %copy.74 = bf16[128,64,2,128]{3,1,2,0:T(8,128)(2,1)} copy(bf16[128,64,2,128]{3,2,1,0:T(2,128)(2,1)} %squeeze.22) | data formatting | bytes 8388608 | tf_op jit(solution)/shard_map/squeeze | solution.py:94
  318.3 3.4 gather_fusion.1
  321.8 1.7 fusion.12
  324.3 1.6 fusion.34
  331.1 2.1 fusion.42
  333.3 3.2 copy.76
  336.5 3.4 gather_fusion.2
  340.0 3.0 fusion.56
  343.3 3.2 convolution_convert_fusion
  346.5 91.8 %reduce-scatter.2.cloned.1.call-done = bf16[512,256]{1,0:T(8,128)(2,1)} async-done(((bf16[512,4096]{1,0:T(8,128)(2,1)}), bf16[512,256]{1,0:T(8,128)(2,1)}) %reduce-scatter.2.cloned.1.call-update) | async-done | bytes 262160 | tf_op jit(solution)/shard_map/reduce_scatter | solution.py:133
  (79 shorter events, 19.5 us)
Async XLA Ops:
  6.5 336.7 %copy-start = (bf16[256,4096]{1,0:T(8,128)(2,1)S(1)}, bf16[256,4096]{1,0:T(8,128)(2,1)}, u32[]{:S(2)}) copy-start(bf16[256,4096]{1,0:T(8,128)(2,1)} %param.8) | copy-start | bytes 6291460
  6.5 68.5 %all-gather.2.cloned.1.call-start = ((), (), s32[]{:S(2)}) async-start(), calls=%async_computation.2 | async-start | bytes 4456448 | tf_op jit(solution)/shard_map/all_gather | solution.py:36
  82.5 0.9 copy-start.10
  87.8 7.4 %copy-start.13 = (s32[2]{0:T(128)S(1)}, s32[2]{0:T(128)}, u32[]{:S(2)}) copy-start(s32[2]{0:T(128)} %param.10) | copy-start | bytes 28
  87.8 7.5 %copy-start.12 = (s32[8,2,3]{0,1,2:T(2,128)S(1)}, s32[8,2,3]{0,1,2:T(2,128)}, u32[]{:S(2)}) copy-start(s32[8,2,3]{0,1,2:T(2,128)} %param.9) | copy-start | bytes 580
  87.8 8.6 %copy-start.14 = (s32[2]{0:T(128)S(1)}, s32[2]{0:T(128)}, u32[]{:S(2)}) copy-start(s32[2]{0:T(128)} %param.11) | copy-start | bytes 28
  87.8 8.7 %copy-start.11 = (bf16[3,512,256]{1,2,0:T(8,128)(2,1)S(1)}, bf16[3,512,256]{1,2,0:T(8,128)(2,1)}, u32[]{:S(2)}) copy-start(bf16[3,512,256]{1,2,0:T(8,128)(2,1)} %copy-done.10) | copy-start | bytes 2359300
  87.8 191.6 %all-to-all-start = ((bf16[16,2,512,256]{3,2,1,0:T(8,128)(2,1)}), bf16[16,2,512,256]{3,2,1,0:T(8,128)(2,1)}, u32[]{:S(2)}, u32[]{:S(2)}) async-start(bf16[16,2,512,256]{3,2,1,0:T(8,128)(2,1)} %stack.10), calls=%async_computation | async-start | bytes 16777216 | tf_op jit(solution)/shard_map/all_to_all | solution.py:83
  95.1 343.2 %reduce-scatter.2.cloned.1.call-start = ((), (), s32[]{:S(2)}) async-start(), calls=%async_computation.3 | async-start | bytes 4456448 | tf_op jit(solution)/shard_map/reduce_scatter | solution.py:133
  97.3 8.0 %collective-permute-start = (bf16[2,64,256]{1,2,0:T(8,128)(2,1)}, bf16[2,64,256]{1,2,0:T(8,128)(2,1)}, u32[]{:S(2)}, u32[]{:S(2)}) collective-permute-start(bf16[2,64,256]{1,2,0:T(8,128)(2,1)} %get-tuple-element.9), channel_id=1, source_target_pairs={{0,16},{16,32},{32,48},{48,64},{64,80},{80,96},{96,112},{112,128},... | collective-permute-start | bytes 196616 | tf_op jit(solution)/shard_map/ppermute | solution.py:17
  100.2 5.1 %collective-permute-start.1 = (bf16[2,64,256]{1,2,0:T(8,128)(2,1)}, bf16[2,64,256]{1,2,0:T(8,128)(2,1)}, u32[]{:S(2)}, u32[]{:S(2)}) collective-permute-start(bf16[2,64,256]{1,2,0:T(8,128)(2,1)} %get-tuple-element.10), channel_id=1, source_target_pairs={{16,0},{32,16},{48,32},{64,48},{80,64},{96,80},{112,96},{128,112},... | collective-permute-start | bytes 196616 | tf_op jit(solution)/shard_map/ppermute | solution.py:20
  104.7 9.1 %copy-start.7 = (bf16[8,64,2,128]{3,2,1,0:T(2,128)(2,1)}, bf16[8,64,2,128]{3,2,1,0:T(2,128)(2,1)S(1)}, u32[]{:S(2)}) copy-start(bf16[8,64,2,128]{3,2,1,0:T(2,128)(2,1)S(1)} %reshape_squeeze.11) | copy-start | bytes 786436
  113.7 1.2 copy-start.8
  114.2 1.2 copy-start.4
  321.8 2.6 copy-start.5
  321.8 2.6 copy-start.9
  323.5 2.5 copy-start.6
  323.5 3.4 copy-start.1
  328.9 2.2 copy-start.3
  331.1 2.2 copy-start.2
Sparse Core Ops, SparseCore 0:
  9.8 65.2 all-gather.1
  346.6 91.6 reduce-scatter.1
